TPU v7x, 128 devices: a whole 4x4x4 slice. The times are simulated.
128 devices in a mesh: row: 16 (over y_hi, x, core), col: 8 (over z, y_lo).
Axes of the slice: x: 4, y: 4 (y_hi: 2, y_lo: 2; y = y_hi * 2 + y_lo), z: 4, core: 2. Of those that a mesh axis runs over, the one named last changes fastest.
Arguments:
- activations: bfloat16 [4, 1024, 8192], P(None, 'col', 'row'), may hold values from -6 to 6
- member_weights: bfloat16 [4, 8192, 1024], P(None, ('col', 'row')), may hold values from -6 to 6
Outputs:
- merged: float32 [8192, 1024], P('row', 'col')
All inputs are finite; a program needn't handle non-finite values.
Results may differ from a plain program's by a relative error of at most 0.0045.
Values may be sent and summed in bfloat16 or wider, within the bound.
A program may use at most 128 MiB of HBM per device.

v0:
```python
import jax
import jax.numpy as jnp
from jax import lax
from jax.sharding import PartitionSpec as P

ITERS = 3


BLEND_WEIGHT = 0.9


def from_root(block, axis, holder):
    block = jnp.where(lax.axis_index(axis) == holder, block, jnp.zeros_like(block))
    return lax.psum(block, axis)


def local(activations, member_weights):
    row_count = lax.axis_size("row")
    col_count = lax.axis_size("col")
    blocks_per = row_count // col_count
    row_index = lax.axis_index("row")
    col_index = lax.axis_index("col")
    token_rows = lax.all_gather(activations, "col", axis=1, tiled=True)
    token_count = token_rows.shape[1]
    row_width = token_rows.shape[2]
    col_width = row_width * blocks_per
    column_list = []
    for which_block in range(blocks_per):
        column_list.append(from_root(token_rows, "row", blocks_per * col_index + which_block))
    column_acts = jnp.concatenate(column_list, axis=2)
    gram_tiles = (
        jnp.einsum("mtr,mtc->mrc", token_rows, column_acts, preferred_element_type=jnp.float32)
        / token_count
    )
    row_ids = row_index * row_width + lax.iota(jnp.int32, row_width)
    col_ids = col_index * col_width + lax.iota(jnp.int32, col_width)
    factor = jnp.where(
        row_ids[:, None] == col_ids[None, :], jnp.float32(1.0), jnp.float32(BLEND_WEIGHT)
    )
    scaled = gram_tiles * factor
    scaled_low = scaled.astype(jnp.bfloat16)
    summed_gram = jnp.sum(scaled, axis=0)
    out_width = member_weights.shape[2]
    partial_rhs = jnp.einsum(
        "mrk,mkd->rd",
        scaled_low,
        lax.all_gather(member_weights, "row", axis=1, tiled=True),
        preferred_element_type=jnp.float32,
    )
    rhs_share = lax.psum_scatter(partial_rhs, "col", scatter_dimension=1, tiled=True)
    right_side = lax.all_gather(rhs_share, "col", axis=1, tiled=True)

    def squares(residual):
        return lax.psum(jnp.sum(residual * residual), "row")

    solution_field = jnp.zeros_like(right_side)
    residual = right_side
    direction = right_side
    norm_now = squares(residual)
    for iteration in range(ITERS):
        column_terms = lax.dot_general(
            summed_gram,
            direction,
            (((0,), (0,)), ((), ())),
            precision=lax.Precision.HIGHEST,
            preferred_element_type=jnp.float32,
        )
        column_share = lax.psum_scatter(column_terms, "row", scatter_dimension=0, tiled=True)
        column_image = lax.all_gather(column_share, "row", axis=0, tiled=True)
        own_half = lax.dynamic_slice_in_dim(
            column_image, row_index % blocks_per * row_width, row_width, 0
        )
        image_out = from_root(own_half, "col", row_index // blocks_per)
        step_size = norm_now / lax.psum(jnp.sum(direction * image_out), "row")
        solution_field = solution_field + step_size * direction
        residual = residual - step_size * image_out
        norm_next = squares(residual)
        direction = residual + norm_next / norm_now * direction
        norm_now = norm_next
    out_group = out_width // col_count
    return lax.dynamic_slice_in_dim(solution_field, col_index * out_group, out_group, 1)


def solution(mesh):
    return jax.shard_map(
        local,
        mesh=mesh,
        in_specs=(P(None, "col", "row"), P(None, ("col", "row"), None)),
        out_specs=P("row", "col"),
        check_vma=False,
    )
```

profile of v0, /device:TPU:1, one launch (start us, length us, event | category | flops | bytes accessed | tf_op | source)
XLA Modules:
  0.0 1433.4 jit_solution(7565898050501885405)
XLA Ops:
  7.3 95.4 %all-gather.7.cloned.1.call-done = bf16[4,1024,512]{2,1,0:T(8,128)(2,1)} async-done(((bf16[4,128,512]{2,1,0:T(8,128)(2,1)}), bf16[4,1024,512]{2,1,0:T(8,128)(2,1)}) %all-gather.7.cloned.1.call-update) | async-done | bytes 4194320 | tf_op jit(solution)/shard_map/all_gather | solution.py:23
  102.7 5.9 broadcast_select_fusion.1
  109.8 161.7 %all-reduce.13.cloned.1.call-done = (bf16[4,1024,512]{2,1,0:T(8,128)(2,1)}, bf16[4,1024,512]{2,1,0:T(8,128)(2,1)}) async-done(((bf16[4,1024,512]{2,1,0:T(8,128)(2,1)}, bf16[4,1024,512]{2,1,0:T(8,128)(2,1)}), (bf16[4,1024,512]{2,1,0:T(8,128)(2,1)}, bf16[4,1024,512]{2,1,0:T(8,128)(2,1)})) %all-reduce.13.cloned.1.call-update) | async-done | bytes 8388624 | tf_op jit(solution)/shard_map/psum | solution.py:14
  271.4 11.3 fusion.4
  282.8 66.1 %all-gather.9.cloned.1.call-done = bf16[4,1024,1024]{2,1,0:T(8,128)(2,1)} async-done(((bf16[4,64,1024]{2,1,0:T(8,128)(2,1)}), bf16[4,1024,1024]{2,1,0:T(8,128)(2,1)}) %all-gather.9.cloned.1.call-update) | async-done | bytes 8388624 | tf_op jit(solution)/shard_map/all_gather | solution.py:47
  348.9 11.7 fusion.9
  360.6 49.9 %reduce-scatter.5.cloned.1.call-done = f32[512,128]{1,0:T(8,128)} async-done(((f32[512,1024]{1,0:T(8,128)}), f32[512,128]{1,0:T(8,128)}) %reduce-scatter.5.cloned.1.call-update) | async-done | bytes 262160 | tf_op jit(solution)/shard_map/reduce_scatter | solution.py:50
  410.6 49.0 %all-gather.11.cloned.1.call-done = f32[512,1024]{1,0:T(8,128)} async-done(((f32[512,128]{1,0:T(8,128)}), f32[512,1024]{1,0:T(8,128)}) %all-gather.11.cloned.1.call-update) | async-done | bytes 2097168 | tf_op jit(solution)/shard_map/all_gather | solution.py:51
  459.6 9.5 fusion.15
  469.1 83.9 %reduce-scatter.7.cloned.1.call-done = f32[64,1024]{1,0:T(8,128)} async-done(((f32[1024,1024]{1,0:T(8,128)}), f32[64,1024]{1,0:T(8,128)}) %reduce-scatter.7.cloned.1.call-update) | async-done | bytes 262160 | tf_op jit(solution)/shard_map/reduce_scatter | solution.py:68
  553.1 59.3 %all-gather.13.cloned.1.call-done = f32[1024,1024]{1,0:T(8,128)} async-done(((f32[64,1024]{1,0:T(8,128)}), f32[1024,1024]{1,0:T(8,128)}) %all-gather.13.cloned.1.call-update) | async-done | bytes 4194320 | tf_op jit(solution)/shard_map/all_gather | solution.py:69
  615.8 102.5 %all-reduce.7.cloned.1.call-done = f32[512,1024]{1,0:T(8,128)} async-done(((f32[512,1024]{1,0:T(8,128)}), f32[512,1024]{1,0:T(8,128)}) %all-reduce.7.cloned.1.call-update) | async-done | bytes 2097168 | tf_op jit(solution)/shard_map/psum | solution.py:14
  721.1 34.6 %all-reduce = (f32[]{:T(128)}, f32[]{:T(128)}) all-reduce(f32[]{:T(128)} %get-tuple-element.6, f32[]{:T(128)} %get-tuple-element.5), channel_id=1, replica_groups=mesh['row'=16,'col'=8] {'row'}, use_global_device_ids=true, to_apply=%region_4.5 | all-reduce | flops 2 | bytes 16 | tf_op jit(solution)/shard_map/psum | solution.py:54
  757.0 4.1 multiply_reduce_fusion.3
  761.0 37.2 %psum.82 = f32[]{:T(128)} all-reduce(f32[]{:T(128)} %get-tuple-element.11), channel_id=1, replica_groups=mesh['row'=16,'col'=8] {'row'}, use_global_device_ids=true, to_apply=%region_11.12 | all-reduce | flops 1 | bytes 8 | tf_op jit(solution)/shard_map/psum | solution.py:54
  803.1 8.2 fusion.16
  811.4 74.6 %reduce-scatter.9.cloned.1.call-done = f32[64,1024]{1,0:T(8,128)} async-done(((f32[1024,1024]{1,0:T(8,128)}), f32[64,1024]{1,0:T(8,128)}) %reduce-scatter.9.cloned.1.call-update) | async-done | bytes 262160 | tf_op jit(solution)/shard_map/reduce_scatter | solution.py:68
  886.1 59.0 %all-gather.15.cloned.1.call-done = f32[1024,1024]{1,0:T(8,128)} async-done(((f32[64,1024]{1,0:T(8,128)}), f32[1024,1024]{1,0:T(8,128)}) %all-gather.15.cloned.1.call-update) | async-done | bytes 4194320 | tf_op jit(solution)/shard_map/all_gather | solution.py:69
  945.2 3.3 dynamic-slice_select_fusion.1
  948.5 102.6 %all-reduce.9.cloned.1.call-done = f32[512,1024]{1,0:T(8,128)} async-done(((f32[512,1024]{1,0:T(8,128)}), f32[512,1024]{1,0:T(8,128)}) %all-reduce.9.cloned.1.call-update) | async-done | bytes 2097168 | tf_op jit(solution)/shard_map/psum | solution.py:14
  1051.2 3.4 multiply_reduce_fusion.2
  1054.5 34.6 %psum.84 = f32[]{:T(128)} all-reduce(f32[]{:T(128)} %multiply_reduce_fusion.2), channel_id=1, replica_groups=mesh['row'=16,'col'=8] {'row'}, use_global_device_ids=true, to_apply=%region_15.16 | all-reduce | flops 1 | bytes 8 | tf_op jit(solution)/shard_map/psum | solution.py:74
  1090.4 3.4 multiply_reduce_fusion.1
  1093.9 37.3 %psum.85 = f32[]{:T(128)} all-reduce(f32[]{:T(128)} %multiply_reduce_fusion.1), channel_id=1, replica_groups=mesh['row'=16,'col'=8] {'row'}, use_global_device_ids=true, to_apply=%region_17.18 | all-reduce | flops 1 | bytes 8 | tf_op jit(solution)/shard_map/psum | solution.py:54
  1132.6 3.7 multiply_add_fusion
  1137.6 8.2 fusion.17
  1145.9 74.6 %reduce-scatter.11.cloned.1.call-done = f32[64,1024]{1,0:T(8,128)} async-done(((f32[1024,1024]{1,0:T(8,128)}), f32[64,1024]{1,0:T(8,128)}) %reduce-scatter.11.cloned.1.call-update) | async-done | bytes 262160 | tf_op jit(solution)/shard_map/reduce_scatter | solution.py:68
  1220.6 59.2 %all-gather.17.cloned.1.call-done = f32[1024,1024]{1,0:T(8,128)} async-done(((f32[64,1024]{1,0:T(8,128)}), f32[1024,1024]{1,0:T(8,128)}) %all-gather.17.cloned.1.call-update) | async-done | bytes 4194320 | tf_op jit(solution)/shard_map/all_gather | solution.py:69
  1279.8 3.3 dynamic-slice_select_fusion
  1283.1 102.7 %all-reduce.11.cloned.1.call-done = f32[512,1024]{1,0:T(8,128)} async-done(((f32[512,1024]{1,0:T(8,128)}), f32[512,1024]{1,0:T(8,128)}) %all-reduce.11.cloned.1.call-update) | async-done | bytes 2097168 | tf_op jit(solution)/shard_map/psum | solution.py:14
  1385.8 3.4 multiply_reduce_fusion
  1389.2 34.6 %psum.87 = f32[]{:T(128)} all-reduce(f32[]{:T(128)} %multiply_reduce_fusion), channel_id=1, replica_groups=mesh['row'=16,'col'=8] {'row'}, use_global_device_ids=true, to_apply=%region_21.22 | all-reduce | flops 1 | bytes 8 | tf_op jit(solution)/shard_map/psum | solution.py:74
  (47 shorter events, 15.2 us)
Async XLA Ops:
  6.5 96.2 %all-gather.7.cloned.1.call-start = ((), (), s32[]{:S(2)}) async-start(), calls=%async_computation.4 | async-start | bytes 4718592 | tf_op jit(solution)/shard_map/all_gather | solution.py:23
  7.3 264.2 %all-reduce.13.cloned.1.call-start = ((), (), s32[]{:S(2)}) async-start(), calls=%async_computation.17 | async-start | bytes 16777216 | tf_op jit(solution)/shard_map/psum | solution.py:14
  108.7 240.2 %all-gather.9.cloned.1.call-start = ((), (), s32[]{:S(2)}) async-start(), calls=%async_computation.5 | async-start | bytes 8912896 | tf_op jit(solution)/shard_map/all_gather | solution.py:47
  109.4 301.1 %reduce-scatter.5.cloned.1.call-start = ((), (), s32[]{:S(2)}) async-start(), calls=%async_computation.6 | async-start | bytes 2359296 | tf_op jit(solution)/shard_map/reduce_scatter | solution.py:50
  360.6 99.1 %copy-start.3 = (f32[512,1024]{0,1:T(8,128)S(1)}, f32[512,1024]{0,1:T(8,128)}, u32[]{:S(2)}) copy-start(f32[512,1024]{0,1:T(8,128)} %get-tuple-element.15) | copy-start | bytes 6291460
  360.6 99.0 %all-gather.11.cloned.1.call-start = ((), (), s32[]{:S(2)}) async-start(), calls=%async_computation.7 | async-start | bytes 2359296 | tf_op jit(solution)/shard_map/all_gather | solution.py:51
  410.6 142.4 %reduce-scatter.7.cloned.1.call-start = ((), (), s32[]{:S(2)}) async-start(), calls=%async_computation.8 | async-start | bytes 4456448 | tf_op jit(solution)/shard_map/reduce_scatter | solution.py:68
  469.1 143.3 %all-gather.13.cloned.1.call-start = ((), (), s32[]{:S(2)}) async-start(), calls=%async_computation.9 | async-start | bytes 4456448 | tf_op jit(solution)/shard_map/all_gather | solution.py:69
  553.0 165.3 %all-reduce.7.cloned.1.call-start = ((), (), s32[]{:S(2)}) async-start(), calls=%async_computation.10 | async-start | bytes 4194304 | tf_op jit(solution)/shard_map/psum | solution.py:14
  615.6 102.7 %copy-start = (f32[512,1024]{1,0:T(8,128)S(1)}, f32[512,1024]{1,0:T(8,128)}, u32[]{:S(2)}) copy-start(f32[512,1024]{1,0:T(8,128)} %all-gather.11.cloned.1.call-done) | copy-start | bytes 6291460
  615.6 270.4 %reduce-scatter.9.cloned.1.call-start = ((), (), s32[]{:S(2)}) async-start(), calls=%async_computation.11 | async-start | bytes 4456448 | tf_op jit(solution)/shard_map/reduce_scatter | solution.py:68
  799.6 3.5 copy-start.4
  801.8 1.3 copy-start.1
  811.4 133.8 %all-gather.15.cloned.1.call-start = ((), (), s32[]{:S(2)}) async-start(), calls=%async_computation.12 | async-start | bytes 4456448 | tf_op jit(solution)/shard_map/all_gather | solution.py:69
  886.1 165.1 %all-reduce.9.cloned.1.call-start = ((), (), s32[]{:S(2)}) async-start(), calls=%async_computation.13 | async-start | bytes 4194304 | tf_op jit(solution)/shard_map/psum | solution.py:14
  948.5 272.0 %reduce-scatter.11.cloned.1.call-start = ((), (), s32[]{:S(2)}) async-start(), calls=%async_computation.14 | async-start | bytes 4456448 | tf_op jit(solution)/shard_map/reduce_scatter | solution.py:68
  1132.5 5.1 copy-start.5
  1136.3 1.3 copy-start.2
  1145.9 133.9 %all-gather.17.cloned.1.call-start = ((), (), s32[]{:S(2)}) async-start(), calls=%async_computation.15 | async-start | bytes 4456448 | tf_op jit(solution)/shard_map/all_gather | solution.py:69
  1220.5 165.3 %all-reduce.11.cloned.1.call-start = ((), (), s32[]{:S(2)}) async-start(), calls=%async_computation.16 | async-start | bytes 4194304 | tf_op jit(solution)/shard_map/psum | solution.py:14
Sparse Core Ops, SparseCore 0:
  9.0 93.6 all-gather.6
  108.8 162.5 all-reduce.12
  273.9 74.8 all-gather.8
  360.7 49.8 reduce-scatter.4
  412.0 47.5 all-gather.10
  469.2 83.7 reduce-scatter.6
  555.4 56.8 all-gather.12
  615.7 102.5 all-reduce.6
  811.5 74.5 reduce-scatter.8
  888.3 56.7 all-gather.14
  948.6 102.5 all-reduce.8
  1146.0 74.4 reduce-scatter.10
  1222.9 56.8 all-gather.16
  1283.2 102.5 all-reduce.10
where the time goes:
time: 1440 us; the launch traced here: 1430 us
  waiting for transfers between devices  1140 us (79%)
  blocking collectives  178 us (12%)
  matrix products  48.9 us (3%)
  other arithmetic  40.7 us (3%)
  between operations  20.1 us (1%)
    psum x4, waiting for transfers between devices, from_root(): return lax.psum(block, axis)  469 us
    reduce_scatter x3, waiting for transfers between devices, local(): lax.psum_scatter(column_terms, 'row', scatter_dimension=0, tiled=True)  233 us
    all_gather x3, waiting for transfers between devices, local(): column_image = lax.all_gather(column_share, 'row', axis=0, tiled=True)  178 us
    psum x3, blocking collectives, squares(): return lax.psum(jnp.sum(residual * residual), 'row')  109 us
    all_gather x1, waiting for transfers between devices, local(): token_rows = lax.all_gather(activations, 'col', axis=1, tiled=True)  95.4 us
    psum x2, blocking collectives, local(): step_size = norm_now / lax.psum(jnp.sum(direction * image_out), 'row')  69.2 us
    all_gather x1, waiting for transfers between devices, local(): lax.all_gather(member_weights, 'row', axis=1, tiled=True)  66.1 us
    reduce_scatter x1, waiting for transfers between devices, local(): lax.psum_scatter(partial_rhs, 'col', scatter_dimension=1, tiled=True)  49.9 us
  transfers between devices with their start and end apart: 14, of which 14 were waited for; matrix products, arithmetic and copies ran while one was open for 1% of the time, Pallas kernels for 0%

commit v1 on v0

v1 whole, which is shorter than its diff:
```python
import jax
import jax.numpy as jnp
from jax import lax
from jax.sharding import PartitionSpec as P

ITERS = 3
BLEND_WEIGHT = 0.9


def local(activations, member_weights):
    rows = lax.axis_size("row")
    cols = lax.axis_size("col")
    per = rows // cols
    row_index = lax.axis_index("row")
    members, tok_block, width = activations.shape
    tokens = tok_block * cols
    out_group = member_weights.shape[2] // cols
    sub = member_weights.shape[1]
    low = jnp.bfloat16

    acts = lax.all_gather(activations, "col", axis=1, tiled=True)
    flat = acts.reshape(members * tokens, width)
    pieces = member_weights.reshape(members, sub, cols, out_group).transpose(2, 0, 1, 3)
    pieces = lax.all_to_all(pieces, "col", 0, 0, tiled=True)
    half = row_index // cols
    slots = jnp.zeros((cols, per) + pieces.shape[1:], low)
    slots = jnp.where(
        lax.broadcasted_iota(jnp.int32, slots.shape, 1) == half, pieces[:, None], slots
    ).reshape((rows,) + pieces.shape[1:])
    got = lax.all_to_all(slots, "row", 0, 0, tiled=True)
    got = got.reshape((per, cols) + pieces.shape[1:])
    got = jnp.where(row_index % per == 0, got[0], got[1])
    weights = got.transpose(1, 0, 2, 3).reshape(members, width, out_group)

    wide = acts.astype(jnp.float32)
    diag = jnp.sum(wide * wide, axis=1) * ((1.0 - BLEND_WEIGHT) / tokens)
    diag_sum = jnp.sum(diag, axis=0)[:, None]
    scale = BLEND_WEIGHT / tokens

    def back(partial):
        share = lax.psum_scatter(partial, "row", scatter_dimension=0, tiled=True)
        full = lax.all_gather(share.astype(low), "row", axis=0, tiled=True)
        return scale * lax.dot_general(
            flat, full, (((0,), (0,)), ((), ())), preferred_element_type=jnp.float32
        )

    def total(*terms):
        return lax.psum(jnp.stack([jnp.sum(a * b) for a, b in terms]), ("row", "col"))

    first = jnp.einsum("mtf,mfd->mtd", acts, weights, preferred_element_type=jnp.float32)
    right_side = back(first.reshape(members * tokens, out_group)) + jnp.sum(
        diag[:, :, None] * weights.astype(jnp.float32), axis=0
    )

    merged = jnp.zeros_like(right_side)
    residual = right_side
    direction = right_side
    norm_now = None
    for iteration in range(ITERS):
        shadow = direction.astype(low)
        partial = jnp.dot(flat, shadow, preferred_element_type=jnp.float32)
        image = back(partial) + diag_sum * direction
        if iteration == 0:
            norm_now, along = total((residual, residual), (direction, image))
        else:
            (along,) = total((direction, image))
        step = norm_now / along
        merged = merged + step * direction
        if iteration + 1 < ITERS:
            residual = residual - step * image
            (norm_next,) = total((residual, residual))
            direction = residual + (norm_next / norm_now) * direction
            norm_now = norm_next
    return merged


def solution(mesh):
    return jax.shard_map(
        local,
        mesh=mesh,
        in_specs=(P(None, "col", "row"), P(None, ("col", "row"), None)),
        out_specs=P("row", "col"),
        check_vma=False,
    )
```

time: 1440 us -> 956 us (0.66)
  waiting for transfers between devices: 1140 us -> 544 us
  blocking collectives: 178 us -> 321 us
  other arithmetic: 40.7 us -> 13.6 us
  starting transfers between devices: 0.7 us -> 18.7 us
  matrix products: 48.9 us -> 31.5 us
    psum x4 -> x0, waiting for transfers between devices: 469 us -> none  [from_root(): return lax.psum(block, axis)]
    psum x5, blocking collectives: 178 us -> 321 us  [total(): lax.psum(jnp.stack([jnp.sum(a * b) for a, b in terms]), ('row', 'col'))]
    all_gather x6 -> x5, waiting for transfers between devices: 388 us -> 248 us  [the longest x4 189 us: back(): full = lax.all_gather(share.astype(low), 'row', axis=0, tiled=True)]
    all_to_all x0 -> x2, waiting for transfers between devices: none -> 27.6 us  [the longest x1 18.4 us: local(): got = lax.all_to_all(slots, 'row', 0, 0, tiled=True)]
    all_to_all x0 -> x2, starting transfers between devices: none -> 18.4 us  [the longest x1 11.5 us: local(): got = lax.all_to_all(slots, 'row', 0, 0, tiled=True)]
    dot_general x5 -> x8, matrix products: 48.9 us -> 31.5 us  [the longest x4 15.1 us: back(): lax.dot_general(flat, full, (((0,), (0,)), ((), ())), preferred_element_t...]
    reduce_scatter x4, waiting for transfers between devices: 283 us -> 267 us  [back(): share = lax.psum_scatter(partial, 'row', scatter_dimension=0, tiled=True)]
    select_n x4 -> x1, other arithmetic: 15.7 us -> 1.11 us  [local(): jnp.where(lax.broadcasted_iota(jnp.int32, slots.shape, 1) == half, pieces...]
  transfers between devices with their start and end apart: 14 -> 11, of which waited for: 14 -> 11; matrix products, arithmetic and copies ran while one was open for 1% -> 0% of each run, Pallas kernels for 0% -> 0%
where the time goes in v1:
time: 956 us; the launch traced here: 955 us
  waiting for transfers between devices  544 us (57%)
  blocking collectives  321 us (34%)
  matrix products  31.5 us (3%)
  between operations  19.9 us (2%)
  starting transfers between devices  18.7 us (2%)
  other arithmetic  13.6 us (1%)
    psum x5, blocking collectives, total(): lax.psum(jnp.stack([jnp.sum(a * b) for a, b in terms]), ('row', 'col'))  321 us
    reduce_scatter x4, waiting for transfers between devices, back(): share = lax.psum_scatter(partial, 'row', scatter_dimension=0, tiled=True)  267 us
    all_gather x4, waiting for transfers between devices, back(): full = lax.all_gather(share.astype(low), 'row', axis=0, tiled=True)  189 us
    all_gather x1, waiting for transfers between devices, local(): acts = lax.all_gather(activations, 'col', axis=1, tiled=True)  59 us
  transfers between devices with their start and end apart: 11, of which 11 were waited for; matrix products, arithmetic and copies ran while one was open for 0% of the time, Pallas kernels for 0%

profile of v1, /device:TPU:1, one launch (start us, length us, event | category | flops | bytes accessed | tf_op | source)
XLA Modules:
  0.0 954.8 jit_solution(12820386908970375079)
XLA Ops:
  9.4 6.9 all-to-all-start
  16.3 9.2 all-to-all-done
  26.6 11.5 %all-to-all-start.1 = ((bf16[16,4,64,128]{3,2,1,0:T(8,128)(2,1)}), bf16[16,4,64,128]{3,2,1,0:T(8,128)(2,1)S(1)}, u32[]{:S(2)}, u32[]{:S(2)}) async-start(bf16[16,4,64,128]{3,2,1,0:T(8,128)(2,1)} %bitcast_select_fusion), calls=%async_computation.1 | async-start | bytes 2097152 | tf_op jit(solution)/shard_map/all_to_all | solution.py:30
  38.2 18.4 %all-to-all-done.1 = bf16[16,4,64,128]{3,2,1,0:T(8,128)(2,1)S(1)} async-done(((bf16[16,4,64,128]{3,2,1,0:T(8,128)(2,1)}), bf16[16,4,64,128]{3,2,1,0:T(8,128)(2,1)S(1)}, u32[]{:S(2)}, u32[]{:S(2)}) %all-to-all-start.1) | async-done | bytes 1048608 | tf_op jit(solution)/shard_map/all_to_all | solution.py:30
  56.8 59.0 %all-gather.6.cloned.1.call-done = bf16[4,1024,512]{2,1,0:T(8,128)(2,1)} async-done(((bf16[4,128,512]{2,1,0:T(8,128)(2,1)}), bf16[4,1024,512]{2,1,0:T(8,128)(2,1)}) %all-gather.6.cloned.1.call-update) | async-done | bytes 4194320 | tf_op jit(solution)/shard_map/all_gather | solution.py:21
  115.7 3.0 multiply_reduce_fusion
  119.2 3.7 convolution_bitcast_fusion.3
  122.9 1.9 copy.20
  124.9 69.2 %reduce-scatter.5.cloned.1.call-done = f32[256,128]{1,0:T(8,128)} async-done(((f32[4096,128]{1,0:T(8,128)}), f32[256,128]{1,0:T(8,128)}) %reduce-scatter.5.cloned.1.call-update) | async-done | bytes 131088 | tf_op jit(solution)/shard_map/reduce_scatter | solution.py:41
  194.1 1.5 convert_element_type.28
  195.8 47.0 %all-gather.8.cloned.1.call-done = bf16[4096,128]{1,0:T(8,128)(2,1)} async-done(((bf16[256,128]{1,0:T(8,128)(2,1)}), bf16[4096,128]{1,0:T(8,128)(2,1)}) %all-gather.8.cloned.1.call-update) | async-done | bytes 1048592 | tf_op jit(solution)/shard_map/all_gather | solution.py:42
  242.8 3.4 fusion.8
  246.5 2.8 convolution_bitcast_fusion.2
  249.4 67.4 %reduce-scatter.7.cloned.1.call-done = f32[256,128]{0,1:T(8,128)} async-done(((f32[4096,128]{0,1:T(8,128)}), f32[256,128]{0,1:T(8,128)}) %reduce-scatter.7.cloned.1.call-update) | async-done | bytes 131088 | tf_op jit(solution)/shard_map/reduce_scatter | solution.py:41
  316.8 1.5 convert_element_type.32
  318.5 47.2 %all-gather.10.cloned.1.call-done = bf16[4096,128]{0,1:T(8,128)(2,1)} async-done(((bf16[256,128]{0,1:T(8,128)(2,1)}), bf16[4096,128]{0,1:T(8,128)(2,1)}) %all-gather.10.cloned.1.call-update) | async-done | bytes 1048592 | tf_op jit(solution)/shard_map/all_gather | solution.py:42
  365.6 3.9 multiply_reduce_fusion.6
  370.9 64.5 %psum.35 = f32[2]{0:T(128)S(1)} all-reduce(f32[2]{0:T(128)S(1)} %pad_maximum_fusion), channel_id=1, replica_groups=mesh['row'=16,'col'=8] {'row','col'}, use_global_device_ids=true, to_apply=%region_7.8 | all-reduce | flops 2 | bytes 16 | tf_op jit(solution)/shard_map/psum | solution.py:48
  437.9 63.8 %psum.36 = f32[1]{0:T(128)} all-reduce(f32[1]{0:T(128)} %bitcast.14), channel_id=1, replica_groups=mesh['row'=16,'col'=8] {'row','col'}, use_global_device_ids=true, to_apply=%region_9.10 | all-reduce | flops 1 | bytes 8 | tf_op jit(solution)/shard_map/psum | solution.py:48
  503.1 5.0 convolution_bitcast_fusion.1
  508.2 65.4 %reduce-scatter.9.cloned.1.call-done = f32[256,128]{0,1:T(8,128)} async-done(((f32[4096,128]{0,1:T(8,128)}), f32[256,128]{0,1:T(8,128)}) %reduce-scatter.9.cloned.1.call-update) | async-done | bytes 131088 | tf_op jit(solution)/shard_map/reduce_scatter | solution.py:41
  573.5 1.5 convert_element_type.34
  575.2 47.3 %all-gather.12.cloned.1.call-done = bf16[4096,128]{0,1:T(8,128)(2,1)} async-done(((bf16[256,128]{0,1:T(8,128)(2,1)}), bf16[4096,128]{0,1:T(8,128)(2,1)}) %all-gather.12.cloned.1.call-update) | async-done | bytes 1048592 | tf_op jit(solution)/shard_map/all_gather | solution.py:42
  622.5 3.9 multiply_reduce_fusion.3
  626.3 64.5 %psum.37 = f32[1]{0:T(128)} all-reduce(f32[1]{0:T(128)} %bitcast.18), channel_id=1, replica_groups=mesh['row'=16,'col'=8] {'row','col'}, use_global_device_ids=true, to_apply=%region_12.13 | all-reduce | flops 1 | bytes 8 | tf_op jit(solution)/shard_map/psum | solution.py:48
  692.9 64.0 %psum.38 = f32[1]{0:T(128)} all-reduce(f32[1]{0:T(128)} %bitcast.20), channel_id=1, replica_groups=mesh['row'=16,'col'=8] {'row','col'}, use_global_device_ids=true, to_apply=%region_14.15 | all-reduce | flops 1 | bytes 8 | tf_op jit(solution)/shard_map/psum | solution.py:48
  758.2 5.0 convolution_bitcast_fusion
  763.3 65.4 %reduce-scatter.11.cloned.1.call-done = f32[256,128]{0,1:T(8,128)} async-done(((f32[4096,128]{0,1:T(8,128)}), f32[256,128]{0,1:T(8,128)}) %reduce-scatter.11.cloned.1.call-update) | async-done | bytes 131088 | tf_op jit(solution)/shard_map/reduce_scatter | solution.py:41
  828.7 1.5 convert_element_type.36
  830.3 47.4 %all-gather.14.cloned.1.call-done = bf16[4096,128]{0,1:T(8,128)(2,1)} async-done(((bf16[256,128]{0,1:T(8,128)(2,1)}), bf16[4096,128]{0,1:T(8,128)(2,1)}) %all-gather.14.cloned.1.call-update) | async-done | bytes 1048592 | tf_op jit(solution)/shard_map/all_gather | solution.py:42
  877.7 3.9 fusion.9
  881.5 64.5 %psum.39 = f32[1]{0:T(128)} all-reduce(f32[1]{0:T(128)} %bitcast.24), channel_id=1, replica_groups=mesh['row'=16,'col'=8] {'row','col'}, use_global_device_ids=true, to_apply=%region_17.18 | all-reduce | flops 1 | bytes 8 | tf_op jit(solution)/shard_map/psum | solution.py:48
  (40 shorter events, 9.8 us)
Async XLA Ops:
  6.5 109.2 %all-gather.6.cloned.1.call-start = ((), (), s32[]{:S(2)}) async-start(), calls=%async_computation.6 | async-start | bytes 4718592 | tf_op jit(solution)/shard_map/all_gather | solution.py:21
  9.4 16.2 %all-to-all-start = ((bf16[8,4,64,128]{3,2,1,0:T(8,128)(2,1)}), bf16[8,4,64,128]{3,2,1,0:T(8,128)(2,1)S(1)}, u32[]{:S(2)}, u32[]{:S(2)}) async-start(bf16[8,4,64,128]{3,2,1,0:T(8,128)(2,1)} %copy.16), calls=%async_computation | async-start | bytes 1048576 | tf_op jit(solution)/shard_map/all_to_all | solution.py:24
  26.6 30.0 %all-to-all-start.1 = ((bf16[16,4,64,128]{3,2,1,0:T(8,128)(2,1)}), bf16[16,4,64,128]{3,2,1,0:T(8,128)(2,1)S(1)}, u32[]{:S(2)}, u32[]{:S(2)}) async-start(bf16[16,4,64,128]{3,2,1,0:T(8,128)(2,1)} %bitcast_select_fusion), calls=%async_computation.1 | async-start | bytes 2097152 | tf_op jit(solution)/shard_map/all_to_all | solution.py:30
  38.2 155.9 %reduce-scatter.5.cloned.1.call-start = ((), (), s32[]{:S(2)}) async-start(), calls=%async_computation.7 | async-start | bytes 2228224 | tf_op jit(solution)/shard_map/reduce_scatter | solution.py:41
  124.8 118.0 %all-gather.8.cloned.1.call-start = ((), (), s32[]{:S(2)}) async-start(), calls=%async_computation.8 | async-start | bytes 1114112 | tf_op jit(solution)/shard_map/all_gather | solution.py:42
  195.6 121.2 %reduce-scatter.7.cloned.1.call-start = ((), (), s32[]{:S(2)}) async-start(), calls=%async_computation.9 | async-start | bytes 2228224 | tf_op jit(solution)/shard_map/reduce_scatter | solution.py:41
  242.8 3.7 copy-start
  249.4 116.3 %all-gather.10.cloned.1.call-start = ((), (), s32[]{:S(2)}) async-start(), calls=%async_computation.10 | async-start | bytes 1114112 | tf_op jit(solution)/shard_map/all_gather | solution.py:42
  318.4 255.1 %reduce-scatter.9.cloned.1.call-start = ((), (), s32[]{:S(2)}) async-start(), calls=%async_computation.11 | async-start | bytes 2228224 | tf_op jit(solution)/shard_map/reduce_scatter | solution.py:41
  508.1 114.4 %all-gather.12.cloned.1.call-start = ((), (), s32[]{:S(2)}) async-start(), calls=%async_computation.12 | async-start | bytes 1114112 | tf_op jit(solution)/shard_map/all_gather | solution.py:42
  575.1 253.6 %reduce-scatter.11.cloned.1.call-start = ((), (), s32[]{:S(2)}) async-start(), calls=%async_computation.13 | async-start | bytes 2228224 | tf_op jit(solution)/shard_map/reduce_scatter | solution.py:41
  763.2 114.4 %all-gather.14.cloned.1.call-start = ((), (), s32[]{:S(2)}) async-start(), calls=%async_computation.14 | async-start | bytes 1114112 | tf_op jit(solution)/shard_map/all_gather | solution.py:42
Sparse Core Ops, SparseCore 0:
  9.0 106.7 all-gather.5
  124.9 69.0 reduce-scatter.4
  196.5 46.2 all-gather.7
  249.5 67.3 reduce-scatter.6
  319.0 46.6 all-gather.9
  508.2 65.2 reduce-scatter.8
  575.8 46.6 all-gather.11
  763.4 65.3 reduce-scatter.10
  831.0 46.6 all-gather.13

commit v2 on v1

v2 whole, which is shorter than its diff:
```python
import jax
import jax.numpy as jnp
from jax import lax
from jax.experimental import pallas as pl
from jax.experimental.pallas import tpu as pltpu
from jax.sharding import PartitionSpec as P

ITERS = 3
BLEND_WEIGHT = 0.9
LOW = jnp.bfloat16
WIDE = jnp.float32
MESH = pl.DeviceIdType.MESH


def dot_nt(a, b):
    return lax.dot_general(a, b, (((1,), (1,)), ((), ())), preferred_element_type=WIDE)


def dot_nn(a, b):
    return lax.dot_general(a, b, (((1,), (0,)), ((), ())), preferred_element_type=WIDE)


def fold(v):
    rows, lanes = v.shape
    v = jnp.sum(v.reshape(rows // 8, 8, lanes), axis=0)
    out = v[:, 0:128]
    for i in range(1, lanes // 128):
        out = out + v[:, 128 * i : 128 * (i + 1)]
    return out


def kernel(
    acts, wts, out,
    xb, wb, wt, dacc, dsum, v, own, psend, precv, pacc, asend, arecv, acc, r, d, x, ex, tile, sa, tile2, sb,
    lsem, xs_sem, xr_sem, fs_sem, fr_sem, ws_sem, wr_sem, wfs_sem, wfr_sem,
    rs_s, rs_r, ag_s, ag_r, s1_s, s1_r, s2_s, s2_r, ex_s, ex_r,
):
    groups, cols = 8, 8
    members, tok = acts.shape[0], acts.shape[1]
    width = acts.shape[2]
    part = v.shape[1]
    scale = BLEND_WEIGHT / (tok * cols)
    dscale = (1.0 - BLEND_WEIGHT) / (tok * cols)

    row = lax.axis_index("row")
    col = lax.axis_index("col")
    g = row // 2
    k = row % 2
    z = col // 2
    y = col % 2
    q = col * 2 + k

    def copy(src, dst, ss, rs, to_row, to_col):
        return pltpu.make_async_remote_copy(
            src_ref=src, dst_ref=dst, send_sem=ss, recv_sem=rs,
            device_id=(to_row, to_col), device_id_type=MESH,
        )

    barrier = pltpu.get_barrier_semaphore()

    def greet(to_row, to_col):
        pl.semaphore_signal(barrier, inc=1, device_id=(to_row, to_col), device_id_type=MESH)

    @pl.loop(1, groups)
    def _(i):
        greet(((g + i) % groups) * 2 + k, col)

    @pl.loop(1, 2 * cols)
    def _(i):
        p = (q + i) % (2 * cols)
        greet(2 * g + p % 2, p // 2)

    @pl.loop(0, cols)
    def _(i):
        @pl.when(jnp.logical_or(col != g, i != col))
        def _():
            greet(2 * col + k, i)

        @pl.when(jnp.logical_or(col != g, i != g))
        def _():
            greet(2 * i + k, g)

    @pl.when(col == g)
    def _():
        pl.semaphore_wait(barrier, 7 + 15 + 14)

    @pl.when(col != g)
    def _():
        pl.semaphore_wait(barrier, 7 + 15 + 16)

    zp = ((z + 1) % 4) * 2
    zm = ((z + 3) % 4) * 2
    zf = ((z + 2) % 4) * 2
    yo = 1 - y
    b_y, b_m, b_p = z * 2 + yo, zm + y, zp + y
    b_my, b_py, b_f, b_fy = zm + yo, zp + yo, zf + y, zf + yo
    c_y, c_p, c_m = z * 2 + yo, zp + y, zm + y
    half = members // 2
    lo, hi = pl.ds(0, half), pl.ds(half, half)
    other = 2 * g + 1 - k

    sends = []

    def start(c):
        c.start()
        sends.append(c)

    def forward(block, n, ms=None):
        ref = xb.at[k, block] if ms is None else xb.at[k, block, ms]
        start(copy(ref, ref, fs_sem.at[n], fr_sem.at[n], other, col))

    local_x = pltpu.make_async_copy(acts, xb.at[k, col], lsem.at[0])
    local_x.start()
    mine = xb.at[k, col]
    start(copy(acts, mine, xs_sem.at[0], xr_sem.at[0], row, c_y))
    start(copy(acts, mine, xs_sem.at[1], xr_sem.at[1], row, c_p))
    start(copy(acts, mine, xs_sem.at[2], xr_sem.at[2], row, c_m))
    start(copy(acts, mine, fs_sem.at[9], fr_sem.at[9], other, col))

    def wcopy(i):
        return copy(
            wts.at[:, :, pl.ds(pl.multiple_of(i * 128, 128), 128)], wb.at[row],
            ws_sem.at[i], wr_sem.at[g], 2 * col + k, i,
        )

    def wlocal():
        return pltpu.make_async_copy(
            wts.at[:, :, pl.ds(pl.multiple_of(col * 128, 128), 128)], wb.at[row], lsem.at[1]
        )

    @pl.loop(0, cols)
    def _(i):
        me = jnp.logical_and(col == g, i == col)

        @pl.when(me)
        def _():
            wlocal().start()

        @pl.when(jnp.logical_not(me))
        def _():
            wcopy(i).start()

    def diag(h, j, first=False):
        for m in range(members):
            t = xb[h, j, m].astype(WIDE)
            t = jnp.sum((t * t).reshape(tok // 8, 8, width), axis=0)
            if first:
                dacc[h, m] = t
            else:
                dacc[h, m] = dacc[h, m] + t

    local_x.wait()

    def fwait(n, block, ms=None):
        ref = xb.at[1 - k, block] if ms is None else xb.at[1 - k, block, ms]
        copy(ref, ref, fs_sem.at[n], fr_sem.at[n], other, col).wait_recv()

    def xwait(n, block, ms=None):
        ref = xb.at[k, block] if ms is None else xb.at[k, block, ms]
        copy(ref, ref, xs_sem.at[0], xr_sem.at[n], row, c_y).wait_recv()

    fwait(9, col)
    diag(0, col, True)
    diag(1, col, True)

    @pl.loop(0, groups)
    def _(i):
        src = 2 * i + k
        me = jnp.logical_and(col == g, i == g)

        @pl.when(me)
        def _():
            wlocal().wait()

        @pl.when(jnp.logical_not(me))
        def _():
            copy(wb.at[src], wb.at[src], ws_sem.at[0], wr_sem.at[i], row, c_y).wait_recv()

        copy(wb.at[src], wb.at[src], wfs_sem.at[i], wfr_sem.at[i], other, col).start()

    @pl.loop(0, groups)
    def _(i):
        src = 2 * i + 1 - k
        copy(wb.at[src], wb.at[src], wfs_sem.at[i], wfr_sem.at[i], other, col).wait_recv()

    for h in range(2):
        for m in range(members):
            w = wb[8 * h : 8 * h + 8, m].reshape(width, 2 * part)
            wt[m, h] = jnp.transpose(w.astype(WIDE)).astype(LOW)

    kpart = pl.ds(pl.multiple_of(k * part, part), part)

    def rs_copy(a, i):
        return copy(
            psend.at[a, i - 1], precv.at[a, i - 1], rs_s.at[a], rs_r.at[a],
            ((g + i) % groups) * 2 + k, col,
        )

    def first_chunk(j):
        i = (j + groups - g) % groups
        for m in range(members):
            t = dot_nt(wt[m, 0, kpart, :], xb[0, j, m]) + dot_nt(wt[m, 1, kpart, :], xb[1, j, m])
            own[:, m * tok : (m + 1) * tok] = t

        @pl.when(j == g)
        def _():
            pacc[...] = own[...]

        @pl.when(j != g)
        def _():
            psend[0, i - 1] = own[...].astype(LOW)
            rs_copy(0, i).start()

    first_chunk(col)

    xwait(0, b_y)
    start(copy(xb.at[k, b_y], xb.at[k, b_y], xs_sem.at[3], xr_sem.at[3], row, c_p))
    start(copy(xb.at[k, b_y], xb.at[k, b_y], xs_sem.at[4], xr_sem.at[4], row, c_m))
    forward(b_y, 0)
    xwait(1, b_m)
    start(copy(xb.at[k, b_m, lo], xb.at[k, b_m, lo], xs_sem.at[5], xr_sem.at[5], row, c_p))
    forward(b_m, 1)
    xwait(2, b_p)
    start(copy(xb.at[k, b_p, hi], xb.at[k, b_p, hi], xs_sem.at[6], xr_sem.at[6], row, c_m))
    forward(b_p, 2)
    for n, b in ((0, b_y), (1, b_m), (2, b_p)):
        fwait(n, b)
        diag(0, b)
        diag(1, b)
        first_chunk(b)
    xwait(5, b_f, lo)
    start(copy(xb.at[k, b_f, lo], xb.at[k, b_f, lo], xs_sem.at[7], xr_sem.at[7], row, c_y))
    forward(b_f, 5, lo)
    xwait(6, b_f, hi)
    start(copy(xb.at[k, b_f, hi], xb.at[k, b_f, hi], xs_sem.at[8], xr_sem.at[8], row, c_y))
    forward(b_f, 6, hi)
    xwait(3, b_my)
    forward(b_my, 3)
    xwait(4, b_py)
    forward(b_py, 4)
    fwait(5, b_f, lo)
    fwait(6, b_f, hi)
    diag(0, b_f)
    diag(1, b_f)
    first_chunk(b_f)
    for n, b in ((3, b_my), (4, b_py)):
        fwait(n, b)
        diag(0, b)
        diag(1, b)
        first_chunk(b)
    xwait(7, b_fy, lo)
    forward(b_fy, 7, lo)
    xwait(8, b_fy, hi)
    forward(b_fy, 8, hi)
    fwait(7, b_fy, lo)
    fwait(8, b_fy, hi)
    diag(0, b_fy)
    diag(1, b_fy)
    first_chunk(b_fy)

    for h in range(2):
        rhs = None
        total = None
        for m in range(members):
            line = jnp.sum(dacc[h, m], axis=0, keepdims=True) * dscale
            term = line * wt[m, h, kpart, :].astype(WIDE)
            rhs = term if rhs is None else rhs + term
            total = line if total is None else total + line
        r[h] = rhs
        dsum[h] = jnp.broadcast_to(total, (8, width))

    def rs_wait(a):
        copy(precv.at[a], precv.at[a], rs_s.at[a], rs_r.at[a], row, c_y).wait_recv()

    def rs_total(a):
        s = precv[a, 0].astype(WIDE)
        for i in range(1, groups - 1):
            s = s + precv[a, i].astype(WIDE)
        return s

    def ag_copy(a, i):
        return copy(
            asend.at[a], arecv.at[a, i - 1], ag_s.at[a, i - 1], ag_r.at[a, i - 1],
            ((g + i) % groups) * 2 + k, col,
        )

    def ag_start(a):
        @pl.loop(1, groups)
        def _(i):
            ag_copy(a, i).start()

    def back_own(a):
        for h in range(2):
            acc[h] = dot_nn(asend[a], xb[h, g].reshape(members * tok, width))

    def back_rest(a):
        @pl.loop(1, groups)
        def _(i):
            j = (g + groups - i) % groups
            ag_copy(a, i).wait_recv()
            p = arecv[a, i - 1]
            for h in range(2):
                acc[h] = acc[h] + dot_nn(p, xb[h, j].reshape(members * tok, width))

    def forth(a):
        def chunk(j):
            return dot_nt(v[0], xb[0, j].reshape(members * tok, width)) + dot_nt(
                v[1], xb[1, j].reshape(members * tok, width)
            )

        @pl.loop(1, groups)
        def _(i):
            psend[a, i - 1] = chunk((g + i) % groups).astype(LOW)
            rs_copy(a, i).start()

        own[...] = chunk(g)

    def s1_copy(e, i):
        return copy(
            tile.at[e], sa.at[e, i - 1], s1_s.at[e, i - 1], s1_r.at[e], ((g + i) % groups) * 2 + k, col
        )

    def s1_start(e):
        @pl.loop(1, groups)
        def _(i):
            s1_copy(e, i).start()

    def s2_copy(e, i):
        p = (q + i) % (2 * cols)
        return copy(
            tile2.at[e], sb.at[e, i - 1], s2_s.at[e, i - 1], s2_r.at[e], 2 * g + p % 2, p // 2
        )

    def s1_finish(e):
        copy(sa.at[e], sa.at[e], s1_s.at[e, 0], s1_r.at[e], row, c_y).wait_recv()
        s = tile[e]
        for i in range(groups - 1):
            s = s + sa[e, i]
        tile2[e] = s

        @pl.loop(1, 2 * cols)
        def _(i):
            s2_copy(e, i).start()

    def s2_finish(e):
        copy(sb.at[e], sb.at[e], s2_s.at[e, 0], s2_r.at[e], row, c_y).wait_recv()
        s = tile2[e]
        for i in range(2 * cols - 1):
            s = s + sb[e, i]
        return s

    rs_wait(0)
    asend[0] = (pacc[...] + rs_total(0)).astype(LOW)
    ag_start(0)
    back_own(0)
    back_rest(0)
    for h in range(2):
        r[h] = r[h] + scale * acc[h]
        d[h] = r[h]
        v[h] = r[h].astype(LOW)
        x[h] = jnp.zeros_like(r[h])

    rr = None
    for it in range(ITERS):
        a = it + 1
        forth(a)
        beta = None
        if it > 0:
            e = 2 * it - 1
            s1_finish(e)
            new = jnp.sum(s2_finish(e)[0])
            beta = new / rr
            rr = new
            for h in range(2):
                d[h] = r[h] + beta * d[h]
        if it == ITERS - 1:
            for n, ref in ((0, x), (1, d)):
                start(copy(ref.at[1 - k], ex.at[n], ex_s.at[n], ex_r.at[n], other, col))
        along = None
        norm = None
        for h in range(2):
            t = fold(d[h] * d[h] * dsum[h, 0:1])
            along = t if along is None else along + t
            if it == 0:
                t = fold(r[h] * r[h])
                norm = t if norm is None else norm + t
        rs_wait(a)
        p = own[...] + rs_total(a)
        if it > 0:
            p = p + beta * pacc[...]
        pacc[...] = p
        e = 2 * it
        if it < ITERS - 1:
            asend[a] = p.astype(LOW)
            ag_start(a)
        tile[e, 0] = along + scale * fold(p * p)
        tile[e, 1] = along if norm is None else norm
        s1_start(e)
        if it < ITERS - 1:
            back_own(a)
        s1_finish(e)
        if it < ITERS - 1:
            back_rest(a)
        s = s2_finish(e)
        if it == 0:
            rr = jnp.sum(s[1])
        alpha = rr / jnp.sum(s[0])
        if it < ITERS - 1:
            norm = None
            for h in range(2):
                image = scale * acc[h] + dsum[h, 0:1] * d[h]
                x[h] = x[h] + alpha * d[h]
                rh = r[h] - alpha * image
                r[h] = rh
                v[h] = rh.astype(LOW)
                t = fold(rh * rh)
                norm = t if norm is None else norm + t
            e = 2 * it + 1
            tile[e, 0] = norm
            tile[e, 1] = norm
            s1_start(e)
        else:
            for n in range(2):
                copy(ex.at[n], ex.at[n], ex_s.at[n], ex_r.at[n], other, col).wait_recv()
            mine_part = x[k] + alpha * d[k]
            other_part = ex[0] + alpha * ex[1]

            @pl.when(k == 0)
            def _():
                out[...] = jnp.transpose(jnp.concatenate([mine_part, other_part], axis=0))

            @pl.when(k == 1)
            def _():
                out[...] = jnp.transpose(jnp.concatenate([other_part, mine_part], axis=0))

    for c in sends:
        c.wait_send()

    @pl.loop(0, cols)
    def _(i):
        @pl.when(jnp.logical_or(col != g, i != col))
        def _():
            wcopy(i).wait_send()

        copy(wb.at[0], wb.at[0], wfs_sem.at[i], wfr_sem.at[i], other, col).wait_send()

    for a in range(ITERS + 1):
        copy(psend.at[a], psend.at[a], rs_s.at[a], rs_r.at[a], row, c_y).wait_send()

    @pl.loop(1, groups)
    def _(i):
        for a in range(ITERS):
            ag_copy(a, i).wait_send()
        for e in range(2 * ITERS - 1):
            s1_copy(e, i).wait_send()

    @pl.loop(1, 2 * cols)
    def _(i):
        for e in range(2 * ITERS - 1):
            s2_copy(e, i).wait_send()


def local(acts, wts):
    members, tok, width = acts.shape
    cols = lax.axis_size("col")
    groups = lax.axis_size("row") // 2
    part = wts.shape[2] // (2 * cols)
    apps = ITERS + 1
    events = 2 * ITERS - 1
    chunk = members * tok
    vmem = pltpu.VMEM
    dma = pltpu.SemaphoreType.DMA
    return pl.pallas_call(
        kernel,
        out_shape=jax.ShapeDtypeStruct((width, 2 * part), WIDE),
        in_specs=[pl.BlockSpec(memory_space=pl.ANY)] * 2,
        out_specs=pl.BlockSpec(memory_space=pltpu.VMEM),
        scratch_shapes=[
            vmem((2, cols, members, tok, width), LOW),
            vmem((2 * groups, members, wts.shape[1], 2 * part), LOW),
            vmem((members, 2, 2 * part, width), LOW),
            vmem((2, members, 8, width), WIDE),
            vmem((2, 8, width), WIDE),
            vmem((2, part, width), LOW),
            vmem((part, chunk), WIDE),
            vmem((apps, groups - 1, part, chunk), LOW),
            vmem((apps, groups - 1, part, chunk), LOW),
            vmem((part, chunk), WIDE),
            vmem((ITERS, part, chunk), LOW),
            vmem((ITERS, groups - 1, part, chunk), LOW),
            vmem((2, part, width), WIDE),
            vmem((2, part, width), WIDE),
            vmem((2, part, width), WIDE),
            vmem((2, part, width), WIDE),
            vmem((2, part, width), WIDE),
            vmem((events, 2, 8, 128), WIDE),
            vmem((events, groups - 1, 2, 8, 128), WIDE),
            vmem((events, 2, 8, 128), WIDE),
            vmem((events, 2 * cols - 1, 2, 8, 128), WIDE),
            dma((2,)),
            dma((9,)),
            dma((9,)),
            dma((10,)),
            dma((10,)),
            dma((cols,)),
            dma((cols,)),
            dma((cols,)),
            dma((cols,)),
            dma((apps,)),
            dma((apps,)),
            dma((ITERS, groups - 1)),
            dma((ITERS, groups - 1)),
            dma((events, groups - 1)),
            dma((events,)),
            dma((events, 2 * cols - 1)),
            dma((events,)),
            dma((2,)),
            dma((2,)),
        ],
        compiler_params=pltpu.CompilerParams(
            collective_id=0, has_side_effects=True, vmem_limit_bytes=60 << 20
        ),
        name="regmean_cg",
    )(acts, wts)


def solution(mesh):
    return jax.shard_map(
        local,
        mesh=mesh,
        in_specs=(P(None, "col", "row"), P(None, ("col", "row"), None)),
        out_specs=P("row", "col"),
        check_vma=False,
    )
```

time: 956 us -> 178 us (0.19)
  waiting for transfers between devices: 544 us -> 0 us
  blocking collectives: 321 us -> 0 us
  Pallas kernels: 0 us -> 176 us
  matrix products: 31.5 us -> 0 us
  between operations: 19.9 us -> 0.01 us
  starting transfers between devices: 18.7 us -> 0 us
  other arithmetic: 13.6 us -> 0 us
    psum x5 -> x0, blocking collectives: 321 us -> none  [total(): lax.psum(jnp.stack([jnp.sum(a * b) for a, b in terms]), ('row', 'col'))]
    reduce_scatter x4 -> x0, waiting for transfers between devices: 267 us -> none  [back(): share = lax.psum_scatter(partial, 'row', scatter_dimension=0, tiled=True)]
    all_gather x5 -> x0, waiting for transfers between devices: 248 us -> none  [the longest x4 189 us: back(): full = lax.all_gather(share.astype(low), 'row', axis=0, tiled=True)]
    pallas_call x0 -> x1, Pallas kernels: none -> 176 us  [local(): pl.pallas_call(kernel, out_shape=jax.ShapeDtypeStruct((width, 2 * part),...]
    dot_general x8 -> x0, matrix products: 31.5 us -> none  [the longest x4 15.1 us: back(): lax.dot_general(flat, full, (((0,), (0,)), ((), ())), preferred_element_t...]
    all_to_all x2 -> x0, waiting for transfers between devices: 27.6 us -> none  [the longest x1 18.4 us: local(): got = lax.all_to_all(slots, 'row', 0, 0, tiled=True)]
    all_to_all x2 -> x0, starting transfers between devices: 18.4 us -> none  [the longest x1 11.5 us: local(): got = lax.all_to_all(slots, 'row', 0, 0, tiled=True)]
  transfers between devices with their start and end apart: 11 -> 0, of which waited for: 11 -> 0; matrix products, arithmetic and copies ran while one was open for 0% -> 0% of each run, Pallas kernels for 0% -> 0%
where the time goes in v2:
time: 178 us
  Pallas kernels  176 us (99%)
    pallas_call x1, Pallas kernels, local(): pl.pallas_call(kernel, out_shape=jax.ShapeDtypeStruct((width, 2 * part),...  176 us

profile of v2, /device:TPU:1, one launch (start us, length us, event | category | flops | bytes accessed | tf_op | source)
XLA Modules:
  0.0 178.0 jit_solution(8935921462944938370)
XLA Ops:
  0.0 176.3 %regmean_cg.1 = f32[512,128]{1,0:T(8,128)} custom-call(bf16[4,128,512]{2,1,0:T(8,128)(2,1)} %acts.1, bf16[4,64,1024]{2,1,0:T(8,128)(2,1)} %wts.1), custom_call_target="tpu_custom_call" | custom-call | tf_op jit(solution)/shard_map/regmean_cg/pallas_call | solution.py:473
  176.3 1.7 copy.4

commit v3 on v2

--- a/solution.py
+++ b/solution.py
@@ -31,8 +31,8 @@
 
 def kernel(
     acts, wts, out,
-    xb, wb, wt, dacc, dsum, v, own, psend, precv, pacc, asend, arecv, acc, r, d, x, ex, tile, sa, tile2, sb,
-    lsem, xs_sem, xr_sem, fs_sem, fr_sem, ws_sem, wr_sem, wfs_sem, wfr_sem,
+    xb, w1, wb, wt, dacc, dsum, v, own, psend, precv, pacc, asend, arecv, acc, r, d, x, ex, tile, sa, tile2, sb,
+    lsem, xs_sem, xr_sem, fs_sem, fr_sem, w1_s, w1_r, w2_s, w2_r, w3_s, w3_r,
     rs_s, rs_r, ag_s, ag_r, s1_s, s1_r, s2_s, s2_r, ex_s, ex_r,
 ):
     groups, cols = 8, 8
@@ -46,6 +46,8 @@
     col = lax.axis_index("col")
     g = row // 2
     k = row % 2
+    x4 = g % 4
+    y2 = g // 4
     z = col // 2
     y = col % 2
     q = col * 2 + k
@@ -56,6 +58,12 @@
             device_id=(to_row, to_col), device_id_type=MESH,
         )
 
+    def peer(i):
+        return ((y2 + i // 4) % 2) * 4 + (x4 + i) % 4
+
+    def source(i):
+        return ((y2 + i // 4) % 2) * 4 + (x4 + 4 - i % 4) % 4
+
     barrier = pltpu.get_barrier_semaphore()
 
     def greet(to_row, to_col):
@@ -63,30 +71,14 @@
 
     @pl.loop(1, groups)
     def _(i):
-        greet(((g + i) % groups) * 2 + k, col)
+        greet(peer(i) * 2 + k, col)
 
     @pl.loop(1, 2 * cols)
     def _(i):
         p = (q + i) % (2 * cols)
         greet(2 * g + p % 2, p // 2)
 
-    @pl.loop(0, cols)
-    def _(i):
-        @pl.when(jnp.logical_or(col != g, i != col))
-        def _():
-            greet(2 * col + k, i)
-
-        @pl.when(jnp.logical_or(col != g, i != g))
-        def _():
-            greet(2 * i + k, g)
-
-    @pl.when(col == g)
-    def _():
-        pl.semaphore_wait(barrier, 7 + 15 + 14)
-
-    @pl.when(col != g)
-    def _():
-        pl.semaphore_wait(barrier, 7 + 15 + 16)
+    pl.semaphore_wait(barrier, 7 + 15)
 
     zp = ((z + 1) % 4) * 2
     zm = ((z + 3) % 4) * 2
@@ -109,6 +101,23 @@
         ref = xb.at[k, block] if ms is None else xb.at[k, block, ms]
         start(copy(ref, ref, fs_sem.at[n], fr_sem.at[n], other, col))
 
+    def w1_src(c):
+        return wts.at[:, :, pl.ds(pl.multiple_of(c * 128, 128), 128)]
+
+    def w1_copy(i):
+        c = ((z + i // 2) % 4) * 2 + (y + i) % 2
+        return copy(w1_src(c), w1.at[col], w1_s.at[i], w1_r.at[i], row, c)
+
+    def w1_from(i):
+        return ((z + 4 - i // 2) % 4) * 2 + (y + i) % 2
+
+    local_w = pltpu.make_async_copy(w1_src(col), w1.at[col], lsem.at[1])
+    local_w.start()
+
+    @pl.loop(1, cols)
+    def _(n):
+        w1_copy(cols - n).start()
+
     local_x = pltpu.make_async_copy(acts, xb.at[k, col], lsem.at[0])
     local_x.start()
     mine = xb.at[k, col]
@@ -116,29 +125,6 @@
     start(copy(acts, mine, xs_sem.at[1], xr_sem.at[1], row, c_p))
     start(copy(acts, mine, xs_sem.at[2], xr_sem.at[2], row, c_m))
     start(copy(acts, mine, fs_sem.at[9], fr_sem.at[9], other, col))
-
-    def wcopy(i):
-        return copy(
-            wts.at[:, :, pl.ds(pl.multiple_of(i * 128, 128), 128)], wb.at[row],
-            ws_sem.at[i], wr_sem.at[g], 2 * col + k, i,
-        )
-
-    def wlocal():
-        return pltpu.make_async_copy(
-            wts.at[:, :, pl.ds(pl.multiple_of(col * 128, 128), 128)], wb.at[row], lsem.at[1]
-        )
-
-    @pl.loop(0, cols)
-    def _(i):
-        me = jnp.logical_and(col == g, i == col)
-
-        @pl.when(me)
-        def _():
-            wlocal().start()
-
-        @pl.when(jnp.logical_not(me))
-        def _():
-            wcopy(i).start()
 
     def diag(h, j, first=False):
         for m in range(members):
@@ -159,29 +145,59 @@
         ref = xb.at[k, block] if ms is None else xb.at[k, block, ms]
         copy(ref, ref, xs_sem.at[0], xr_sem.at[n], row, c_y).wait_recv()
 
+    def relay(n, block, to, ms=None):
+        ref = xb.at[k, block] if ms is None else xb.at[k, block, ms]
+        start(copy(ref, ref, xs_sem.at[n], xr_sem.at[n], row, to))
+
+    def w2_copy(i):
+        p = peer(i)
+        return copy(w1.at[p], wb.at[row], w2_s.at[i], w2_r.at[i], 2 * p + k, col)
+
+    def w2_forward(i):
+        ref = wb.at[2 * source(i) + k]
+        return copy(ref, ref, w3_s.at[i], w3_r.at[i], other, col)
+
+    local_w.wait()
+
+    @pl.loop(1, cols)
+    def _(n):
+        i = cols - n
+        ref = w1.at[w1_from(i)]
+        copy(ref, ref, w1_s.at[i], w1_r.at[i], row, c_y).wait_recv()
+
+    @pl.loop(1, groups)
+    def _(n):
+        w2_copy(groups - n).start()
+
+    own_w = pltpu.make_async_copy(w1.at[g], wb.at[row], lsem.at[1])
+    own_w.start()
     fwait(9, col)
     diag(0, col, True)
     diag(1, col, True)
+    own_w.wait()
+    w2_forward(0).start()
+    xwait(1, b_m)
+    relay(5, b_m, c_p, lo)
+    forward(b_m, 1)
+    xwait(2, b_p)
+    relay(6, b_p, c_m, hi)
+    forward(b_p, 2)
+    xwait(0, b_y)
+    relay(3, b_y, c_p)
+    relay(4, b_y, c_m)
+    forward(b_y, 0)
+
+    @pl.loop(1, groups)
+    def _(n):
+        i = groups - n
+        ref = wb.at[2 * source(i) + k]
+        copy(ref, ref, w2_s.at[i], w2_r.at[i], row, c_y).wait_recv()
+        w2_forward(i).start()
 
     @pl.loop(0, groups)
     def _(i):
-        src = 2 * i + k
-        me = jnp.logical_and(col == g, i == g)
-
-        @pl.when(me)
-        def _():
-            wlocal().wait()
-
-        @pl.when(jnp.logical_not(me))
-        def _():
-            copy(wb.at[src], wb.at[src], ws_sem.at[0], wr_sem.at[i], row, c_y).wait_recv()
-
-        copy(wb.at[src], wb.at[src], wfs_sem.at[i], wfr_sem.at[i], other, col).start()
-
-    @pl.loop(0, groups)
-    def _(i):
-        src = 2 * i + 1 - k
-        copy(wb.at[src], wb.at[src], wfs_sem.at[i], wfr_sem.at[i], other, col).wait_recv()
+        ref = wb.at[2 * source(i) + 1 - k]
+        copy(ref, ref, w3_s.at[i], w3_r.at[i], other, col).wait_recv()
 
     for h in range(2):
         for m in range(members):
@@ -193,11 +209,11 @@
     def rs_copy(a, i):
         return copy(
             psend.at[a, i - 1], precv.at[a, i - 1], rs_s.at[a], rs_r.at[a],
-            ((g + i) % groups) * 2 + k, col,
+            peer(i) * 2 + k, col,
         )
 
     def first_chunk(j):
-        i = (j + groups - g) % groups
+        i = ((j // 4 + y2) % 2) * 4 + (j + 4 - x4) % 4
         for m in range(members):
             t = dot_nt(wt[m, 0, kpart, :], xb[0, j, m]) + dot_nt(wt[m, 1, kpart, :], xb[1, j, m])
             own[:, m * tok : (m + 1) * tok] = t
@@ -211,52 +227,39 @@
             psend[0, i - 1] = own[...].astype(LOW)
             rs_copy(0, i).start()
 
+    def use(block):
+        first_chunk(block)
+        diag(0, block)
+        diag(1, block)
+
     first_chunk(col)
-
-    xwait(0, b_y)
-    start(copy(xb.at[k, b_y], xb.at[k, b_y], xs_sem.at[3], xr_sem.at[3], row, c_p))
-    start(copy(xb.at[k, b_y], xb.at[k, b_y], xs_sem.at[4], xr_sem.at[4], row, c_m))
-    forward(b_y, 0)
-    xwait(1, b_m)
-    start(copy(xb.at[k, b_m, lo], xb.at[k, b_m, lo], xs_sem.at[5], xr_sem.at[5], row, c_p))
-    forward(b_m, 1)
-    xwait(2, b_p)
-    start(copy(xb.at[k, b_p, hi], xb.at[k, b_p, hi], xs_sem.at[6], xr_sem.at[6], row, c_m))
-    forward(b_p, 2)
     for n, b in ((0, b_y), (1, b_m), (2, b_p)):
         fwait(n, b)
-        diag(0, b)
-        diag(1, b)
-        first_chunk(b)
+        use(b)
     xwait(5, b_f, lo)
-    start(copy(xb.at[k, b_f, lo], xb.at[k, b_f, lo], xs_sem.at[7], xr_sem.at[7], row, c_y))
+    relay(7, b_f, c_y, lo)
     forward(b_f, 5, lo)
     xwait(6, b_f, hi)
-    start(copy(xb.at[k, b_f, hi], xb.at[k, b_f, hi], xs_sem.at[8], xr_sem.at[8], row, c_y))
+    relay(8, b_f, c_y, hi)
     forward(b_f, 6, hi)
+    fwait(5, b_f, lo)
+    fwait(6, b_f, hi)
+    use(b_f)
     xwait(3, b_my)
     forward(b_my, 3)
     xwait(4, b_py)
     forward(b_py, 4)
-    fwait(5, b_f, lo)
-    fwait(6, b_f, hi)
-    diag(0, b_f)
-    diag(1, b_f)
-    first_chunk(b_f)
-    for n, b in ((3, b_my), (4, b_py)):
-        fwait(n, b)
-        diag(0, b)
-        diag(1, b)
-        first_chunk(b)
     xwait(7, b_fy, lo)
     forward(b_fy, 7, lo)
     xwait(8, b_fy, hi)
     forward(b_fy, 8, hi)
+    fwait(3, b_my)
+    use(b_my)
+    fwait(4, b_py)
+    use(b_py)
     fwait(7, b_fy, lo)
     fwait(8, b_fy, hi)
-    diag(0, b_fy)
-    diag(1, b_fy)
-    first_chunk(b_fy)
+    use(b_fy)
 
     for h in range(2):
         rhs = None
@@ -281,13 +284,13 @@
     def ag_copy(a, i):
         return copy(
             asend.at[a], arecv.at[a, i - 1], ag_s.at[a, i - 1], ag_r.at[a, i - 1],
-            ((g + i) % groups) * 2 + k, col,
+            peer(i) * 2 + k, col,
         )
 
     def ag_start(a):
         @pl.loop(1, groups)
-        def _(i):
-            ag_copy(a, i).start()
+        def _(n):
+            ag_copy(a, groups - n).start()
 
     def back_own(a):
         for h in range(2):
@@ -295,8 +298,9 @@
 
     def back_rest(a):
         @pl.loop(1, groups)
-        def _(i):
-            j = (g + groups - i) % groups
+        def _(n):
+            i = groups - n
+            j = source(i)
             ag_copy(a, i).wait_recv()
             p = arecv[a, i - 1]
             for h in range(2):
@@ -309,15 +313,16 @@
             )
 
         @pl.loop(1, groups)
-        def _(i):
-            psend[a, i - 1] = chunk((g + i) % groups).astype(LOW)
+        def _(n):
+            i = groups - n
+            psend[a, i - 1] = chunk(peer(i)).astype(LOW)
             rs_copy(a, i).start()
 
         own[...] = chunk(g)
 
     def s1_copy(e, i):
         return copy(
-            tile.at[e], sa.at[e, i - 1], s1_s.at[e, i - 1], s1_r.at[e], ((g + i) % groups) * 2 + k, col
+            tile.at[e], sa.at[e, i - 1], s1_s.at[e, i - 1], s1_r.at[e], peer(i) * 2 + k, col
         )
 
     def s1_start(e):
@@ -390,13 +395,12 @@
             p = p + beta * pacc[...]
         pacc[...] = p
         e = 2 * it
-        if it < ITERS - 1:
-            asend[a] = p.astype(LOW)
-            ag_start(a)
         tile[e, 0] = along + scale * fold(p * p)
         tile[e, 1] = along if norm is None else norm
         s1_start(e)
         if it < ITERS - 1:
+            asend[a] = p.astype(LOW)
+            ag_start(a)
             back_own(a)
         s1_finish(e)
         if it < ITERS - 1:
@@ -436,13 +440,14 @@
     for c in sends:
         c.wait_send()
 
-    @pl.loop(0, cols)
-    def _(i):
-        @pl.when(jnp.logical_or(col != g, i != col))
-        def _():
-            wcopy(i).wait_send()
-
-        copy(wb.at[0], wb.at[0], wfs_sem.at[i], wfr_sem.at[i], other, col).wait_send()
+    @pl.loop(1, cols)
+    def _(i):
+        w1_copy(i).wait_send()
+        w2_copy(i).wait_send()
+
+    @pl.loop(0, groups)
+    def _(i):
+        w2_forward(i).wait_send()
 
     for a in range(ITERS + 1):
         copy(psend.at[a], psend.at[a], rs_s.at[a], rs_r.at[a], row, c_y).wait_send()
@@ -477,6 +482,7 @@
         out_specs=pl.BlockSpec(memory_space=pltpu.VMEM),
         scratch_shapes=[
             vmem((2, cols, members, tok, width), LOW),
+            vmem((cols, members, wts.shape[1], 2 * part), LOW),
             vmem((2 * groups, members, wts.shape[1], 2 * part), LOW),
             vmem((members, 2, 2 * part, width), LOW),
             vmem((2, members, 8, width), WIDE),
@@ -504,8 +510,10 @@
             dma((10,)),
             dma((cols,)),
             dma((cols,)),
-            dma((cols,)),
-            dma((cols,)),
+            dma((groups,)),
+            dma((groups,)),
+            dma((groups,)),
+            dma((groups,)),
             dma((apps,)),
             dma((apps,)),
             dma((ITERS, groups - 1)),

time: 178 us -> 144 us (0.81)
  Pallas kernels: 176 us -> 142 us
    pallas_call x1, Pallas kernels: 176 us -> 142 us  [local(): pl.pallas_call(kernel, out_shape=jax.ShapeDtypeStruct((width, 2 * part),...]
where the time goes in v3:
time: 144 us
  Pallas kernels  142 us (99%)
  local copies, waits for them, and re-layouts  1.67 us (1%)
    pallas_call x1, Pallas kernels, local(): pl.pallas_call(kernel, out_shape=jax.ShapeDtypeStruct((width, 2 * part),...  142 us

profile of v3, /device:TPU:1, one launch (start us, length us, event | category | flops | bytes accessed | tf_op | source)
XLA Modules:
  0.0 143.5 jit_solution(2612673827265911163)
XLA Ops:
  0.0 141.8 %regmean_cg.1 = f32[512,128]{1,0:T(8,128)} custom-call(bf16[4,128,512]{2,1,0:T(8,128)(2,1)} %acts.1, bf16[4,64,1024]{2,1,0:T(8,128)(2,1)} %wts.1), custom_call_target="tpu_custom_call" | custom-call | tf_op jit(solution)/shard_map/regmean_cg/pallas_call | solution.py:478
  141.9 1.7 %copy.4 = f32[512,128]{1,0:T(8,128)} copy(f32[512,128]{1,0:T(8,128)} %regmean_cg.1) | data formatting | bytes 524288

commit v4 on v3

--- a/solution.py
+++ b/solution.py
@@ -44,12 +44,12 @@
 
     row = lax.axis_index("row")
     col = lax.axis_index("col")
-    g = row // 2
-    k = row % 2
-    x4 = g % 4
-    y2 = g // 4
-    z = col // 2
-    y = col % 2
+    g = lax.div(row, 2)
+    k = lax.rem(row, 2)
+    x4 = lax.rem(g, 4)
+    y2 = lax.div(g, 4)
+    z = lax.div(col, 2)
+    y = lax.rem(col, 2)
     q = col * 2 + k
 
     def copy(src, dst, ss, rs, to_row, to_col):
@@ -59,30 +59,39 @@
         )
 
     def peer(i):
-        return ((y2 + i // 4) % 2) * 4 + (x4 + i) % 4
+        return (lax.rem(y2 + i // 4, 2)) * 4 + lax.rem(x4 + i, 4)
 
     def source(i):
-        return ((y2 + i // 4) % 2) * 4 + (x4 + 4 - i % 4) % 4
+        return (lax.rem(y2 + i // 4, 2)) * 4 + lax.rem(x4 + 4 - i % 4, 4)
+
+    yp = 2 * y2 + y
+
+    def plane(i):
+        t = lax.rem(yp + i // 4, 4)
+        return (lax.div(t, 2) * 4 + lax.rem(x4 + i, 4)) * 2 + k, z * 2 + lax.rem(t, 2)
+
+    def pole(i):
+        return 2 * g + lax.rem(k + i, 2), lax.rem(z + i // 2, 4) * 2 + y
 
     barrier = pltpu.get_barrier_semaphore()
 
     def greet(to_row, to_col):
         pl.semaphore_signal(barrier, inc=1, device_id=(to_row, to_col), device_id_type=MESH)
 
-    @pl.loop(1, groups)
-    def _(i):
-        greet(peer(i) * 2 + k, col)
+    @pl.loop(1, 2 * groups)
+    def _(i):
+        greet(*plane(i))
 
     @pl.loop(1, 2 * cols)
     def _(i):
-        p = (q + i) % (2 * cols)
-        greet(2 * g + p % 2, p // 2)
-
-    pl.semaphore_wait(barrier, 7 + 15)
-
-    zp = ((z + 1) % 4) * 2
-    zm = ((z + 3) % 4) * 2
-    zf = ((z + 2) % 4) * 2
+        p = lax.rem(q + i, 2 * cols)
+        greet(2 * g + lax.rem(p, 2), lax.div(p, 2))
+
+    pl.semaphore_wait(barrier, 15 + 15)
+
+    zp = lax.rem(z + 1, 4) * 2
+    zm = lax.rem(z + 3, 4) * 2
+    zf = lax.rem(z + 2, 4) * 2
     yo = 1 - y
     b_y, b_m, b_p = z * 2 + yo, zm + y, zp + y
     b_my, b_py, b_f, b_fy = zm + yo, zp + yo, zf + y, zf + yo
@@ -105,11 +114,11 @@
         return wts.at[:, :, pl.ds(pl.multiple_of(c * 128, 128), 128)]
 
     def w1_copy(i):
-        c = ((z + i // 2) % 4) * 2 + (y + i) % 2
+        c = lax.rem(z + i // 2, 4) * 2 + lax.rem(y + i, 2)
         return copy(w1_src(c), w1.at[col], w1_s.at[i], w1_r.at[i], row, c)
 
     def w1_from(i):
-        return ((z + 4 - i // 2) % 4) * 2 + (y + i) % 2
+        return lax.rem(z + 4 - i // 2, 4) * 2 + lax.rem(y + i, 2)
 
     local_w = pltpu.make_async_copy(w1_src(col), w1.at[col], lsem.at[1])
     local_w.start()
@@ -122,8 +131,8 @@
     local_x.start()
     mine = xb.at[k, col]
     start(copy(acts, mine, xs_sem.at[0], xr_sem.at[0], row, c_y))
-    start(copy(acts, mine, xs_sem.at[1], xr_sem.at[1], row, c_p))
-    start(copy(acts, mine, xs_sem.at[2], xr_sem.at[2], row, c_m))
+    for n, to, ms in ((1, c_p, lo), (2, c_m, hi), (9, c_p, hi), (10, c_m, lo)):
+        start(copy(acts.at[ms], xb.at[k, col, ms], xs_sem.at[n], xr_sem.at[n], row, to))
     start(copy(acts, mine, fs_sem.at[9], fr_sem.at[9], other, col))
 
     def diag(h, j, first=False):
@@ -176,16 +185,18 @@
     diag(1, col, True)
     own_w.wait()
     w2_forward(0).start()
-    xwait(1, b_m)
+    xwait(1, b_m, lo)
     relay(5, b_m, c_p, lo)
-    forward(b_m, 1)
-    xwait(2, b_p)
+    xwait(2, b_p, hi)
     relay(6, b_p, c_m, hi)
-    forward(b_p, 2)
     xwait(0, b_y)
     relay(3, b_y, c_p)
     relay(4, b_y, c_m)
     forward(b_y, 0)
+    xwait(9, b_m, hi)
+    forward(b_m, 1)
+    xwait(10, b_p, lo)
+    forward(b_p, 2)
 
     @pl.loop(1, groups)
     def _(n):
@@ -213,7 +224,7 @@
         )
 
     def first_chunk(j):
-        i = ((j // 4 + y2) % 2) * 4 + (j + 4 - x4) % 4
+        i = lax.rem(lax.div(j, 4) + y2, 2) * 4 + lax.rem(j + 4 - x4, 4)
         for m in range(members):
             t = dot_nt(wt[m, 0, kpart, :], xb[0, j, m]) + dot_nt(wt[m, 1, kpart, :], xb[1, j, m])
             own[:, m * tok : (m + 1) * tok] = t
@@ -232,19 +243,19 @@
         diag(0, block)
         diag(1, block)
 
-    first_chunk(col)
-    for n, b in ((0, b_y), (1, b_m), (2, b_p)):
-        fwait(n, b)
-        use(b)
     xwait(5, b_f, lo)
     relay(7, b_f, c_y, lo)
     forward(b_f, 5, lo)
     xwait(6, b_f, hi)
     relay(8, b_f, c_y, hi)
     forward(b_f, 6, hi)
+    first_chunk(col)
+    for n, b in ((0, b_y), (1, b_m), (2, b_p)):
+        fwait(n, b)
+        use(b)
     fwait(5, b_f, lo)
     fwait(6, b_f, hi)
-    use(b_f)
+    first_chunk(b_f)
     xwait(3, b_my)
     forward(b_my, 3)
     xwait(4, b_py)
@@ -254,12 +265,15 @@
     xwait(8, b_fy, hi)
     forward(b_fy, 8, hi)
     fwait(3, b_my)
-    use(b_my)
+    first_chunk(b_my)
     fwait(4, b_py)
-    use(b_py)
+    first_chunk(b_py)
     fwait(7, b_fy, lo)
     fwait(8, b_fy, hi)
-    use(b_fy)
+    first_chunk(b_fy)
+    for b in (b_f, b_my, b_py, b_fy):
+        diag(0, b)
+        diag(1, b)
 
     for h in range(2):
         rhs = None
@@ -321,36 +335,31 @@
         own[...] = chunk(g)
 
     def s1_copy(e, i):
-        return copy(
-            tile.at[e], sa.at[e, i - 1], s1_s.at[e, i - 1], s1_r.at[e], peer(i) * 2 + k, col
-        )
+        return copy(tile.at[e], sa.at[e, i - 1], s1_s.at[e, i - 1], s1_r.at[e], *pole(i))
 
     def s1_start(e):
-        @pl.loop(1, groups)
-        def _(i):
-            s1_copy(e, i).start()
+        @pl.loop(1, cols)
+        def _(n):
+            s1_copy(e, cols - n).start()
 
     def s2_copy(e, i):
-        p = (q + i) % (2 * cols)
-        return copy(
-            tile2.at[e], sb.at[e, i - 1], s2_s.at[e, i - 1], s2_r.at[e], 2 * g + p % 2, p // 2
-        )
+        return copy(tile2.at[e], sb.at[e, i - 1], s2_s.at[e, i - 1], s2_r.at[e], *plane(i))
 
     def s1_finish(e):
         copy(sa.at[e], sa.at[e], s1_s.at[e, 0], s1_r.at[e], row, c_y).wait_recv()
         s = tile[e]
-        for i in range(groups - 1):
+        for i in range(cols - 1):
             s = s + sa[e, i]
         tile2[e] = s
 
-        @pl.loop(1, 2 * cols)
-        def _(i):
-            s2_copy(e, i).start()
+        @pl.loop(1, 2 * groups)
+        def _(n):
+            s2_copy(e, 2 * groups - n).start()
 
     def s2_finish(e):
         copy(sb.at[e], sb.at[e], s2_s.at[e, 0], s2_r.at[e], row, c_y).wait_recv()
         s = tile2[e]
-        for i in range(2 * cols - 1):
+        for i in range(2 * groups - 1):
             s = s + sb[e, i]
         return s
 
@@ -459,7 +468,7 @@
         for e in range(2 * ITERS - 1):
             s1_copy(e, i).wait_send()
 
-    @pl.loop(1, 2 * cols)
+    @pl.loop(1, 2 * groups)
     def _(i):
         for e in range(2 * ITERS - 1):
             s2_copy(e, i).wait_send()
@@ -500,12 +509,12 @@
             vmem((2, part, width), WIDE),
             vmem((2, part, width), WIDE),
             vmem((events, 2, 8, 128), WIDE),
-            vmem((events, groups - 1, 2, 8, 128), WIDE),
+            vmem((events, cols - 1, 2, 8, 128), WIDE),
             vmem((events, 2, 8, 128), WIDE),
-            vmem((events, 2 * cols - 1, 2, 8, 128), WIDE),
+            vmem((events, 2 * groups - 1, 2, 8, 128), WIDE),
             dma((2,)),
-            dma((9,)),
-            dma((9,)),
+            dma((11,)),
+            dma((11,)),
             dma((10,)),
             dma((10,)),
             dma((cols,)),
@@ -518,9 +527,9 @@
             dma((apps,)),
             dma((ITERS, groups - 1)),
             dma((ITERS, groups - 1)),
-            dma((events, groups - 1)),
+            dma((events, cols - 1)),
             dma((events,)),
-            dma((events, 2 * cols - 1)),
+            dma((events, 2 * groups - 1)),
             dma((events,)),
             dma((2,)),
             dma((2,)),

time: 144 us -> 135 us (0.938)
  Pallas kernels: 142 us -> 133 us
    pallas_call x1, Pallas kernels: 142 us -> 133 us  [local(): pl.pallas_call(kernel, out_shape=jax.ShapeDtypeStruct((width, 2 * part),...]
where the time goes in v4:
time: 135 us
  Pallas kernels  133 us (99%)
  local copies, waits for them, and re-layouts  1.67 us (1%)
    pallas_call x1, Pallas kernels, local(): pl.pallas_call(kernel, out_shape=jax.ShapeDtypeStruct((width, 2 * part),...  133 us

profile of v4, /device:TPU:1, one launch (start us, length us, event | category | flops | bytes accessed | tf_op | source)
XLA Modules:
  0.0 134.7 jit_solution(12033632454520617000)
XLA Ops:
  0.0 133.0 %regmean_cg.1 = f32[512,128]{1,0:T(8,128)} custom-call(bf16[4,128,512]{2,1,0:T(8,128)(2,1)} %acts.1, bf16[4,64,1024]{2,1,0:T(8,128)(2,1)} %wts.1), custom_call_target="tpu_custom_call" | custom-call | tf_op jit(solution)/shard_map/regmean_cg/pallas_call | solution.py:487
  133.0 1.7 %copy.4 = f32[512,128]{1,0:T(8,128)} copy(f32[512,128]{1,0:T(8,128)} %regmean_cg.1) | data formatting | bytes 524288
